TPU v7x, 1024 devices: a whole 8x8x8 slice. The times are simulated.
1024 devices in a mesh: wide: 128 (over x, z, core), lend: 8 (over y).
Axes of the slice: x: 8, y: 8, z: 8, core: 2. Of those that a mesh axis runs over, the one named last changes fastest.
Arguments:
- operators: bfloat16 [8, 128, 1024, 1024], P('lend', 'wide'), as said below
- dual_rhs: float32 [8, 65536, 128], P('lend', 'wide'), may hold values from -6 to 6
- contact: int32 [8, 65536], P('lend', 'wide'), may hold values 0 or 1
- costs: int32 [8, 128], P('lend', 'wide'), may hold values from 1 to 8, as said below
Outputs:
- multipliers: float32 [8, 65536, 128], P('lend', 'wide')
- gradient: float32 [8, 65536, 128], P('lend', 'wide')
Inputs may be any that keep to these rules, and one draw needn't show every extreme that they name: `operators`: each subdomain's operator is symmetric positive definite up to rounding. 1 marks a contact multiplier that must stay nonnegative, 0 a gluing one. The number of live blocks of 128 slots of each subdomain; its live slots are the first costs * 128. For every j, costs[2 j, w] + costs[2 j + 1, w] is at most 9.
All inputs are finite; a program needn't handle non-finite values. No bound on the sum of `contact` on one device may be relied on, other than what follows from the above.
Results may differ from a plain program's by a relative error of at most 0.0086.
Values may be sent and summed in bfloat16 or wider, within the bound.
No kernel may reach another device: no remote copies, remote signals or barrier semaphores. Data moves between devices by JAX's collectives and lax.ppermute only.
A program may use at most 32 MiB of HBM per device.

v0:
```python
import functools

import jax
import jax.numpy as jnp
from jax import lax
from jax.experimental import pallas as pl
from jax.experimental.pallas import tpu as pltpu
from jax.sharding import Mesh
from jax.sharding import PartitionSpec as P


ROWBLK = 128
ITERS = 4
RIDGE = 1.0
FIRST_STEP = 0.1
EPSILON = 1e-6
CHUNK = 128
TILE = 256
EXTRA = 8
WIDE = ("chip", "core")

HBM = pl.BlockSpec(memory_space=pltpu.HBM)
VMEM = pl.BlockSpec(memory_space=pltpu.VMEM)
SMEM = pl.BlockSpec(memory_space=pltpu.SMEM)


def base_of(par, half, face):
    return face * ((1 - par) if half == 0 else par)


def sign_of(par, half):
    return jnp.where((par == 0) == (half == 0), 1.0, -1.0)


def fold(values):
    return jnp.sum(values.reshape(values.shape[0] // 8, 8, values.shape[1]), axis=0)


def set_face(rhs, flags, base, g_ref, lo_ref):
    for t in range(rhs.shape[0] // CHUNK):
        off = pl.multiple_of(base + t * CHUNK, CHUNK)
        row = flags[0:1, t * CHUNK:(t + 1) * CHUNK].astype(jnp.float32)
        column = jnp.broadcast_to(row, (CHUNK, CHUNK)).T
        lo_ref[pl.ds(off, CHUNK), :] = jnp.where(column == 1.0, 0.0, -jnp.inf).astype(lo_ref.dtype)
        g_ref[pl.ds(off, CHUNK), :] = -rhs[pl.ds(t * CHUNK, CHUNK), :]


def store_operand(par, live, chunk, change, face, u_ref):
    half = (chunk * CHUNK) // face
    off = pl.multiple_of(base_of(par, half, face) + chunk * CHUNK - half * face, CHUNK)
    slots = off + lax.broadcasted_iota(jnp.int32, change.shape, 0)
    kept = jnp.where(slots < live * ROWBLK, change * sign_of(par, half), 0.0)
    u_ref[pl.ds(off, CHUNK), :] = kept.astype(jnp.bfloat16)


def tile_product(off, live, k_ref, operand):
    off = pl.multiple_of(off, TILE)
    piece = jnp.dot(k_ref[pl.ds(off, TILE), :], operand, preferred_element_type=jnp.float32)
    slots = off + lax.broadcasted_iota(jnp.int32, piece.shape, 0)
    return jnp.where(slots < live * ROWBLK, piece, 0.0)


def product(par, live, squares, k_ref, u_ref, g_ref, c_ref, q_ref, near_ref, far_ref):
    face = far_ref.shape[0]
    operand = u_ref[...]
    denom = jnp.zeros((8, c_ref.shape[1]), jnp.float32)
    for half in range(2):
        sign = sign_of(par, half)
        total = jnp.zeros_like(denom)
        for t in range(face // TILE):
            piece = tile_product(base_of(par, half, face) + t * TILE, live, k_ref, operand)
            rows = pl.ds(half * face + t * TILE, TILE)
            (near_ref, far_ref)[half][pl.ds(t * TILE, TILE), :] = piece
            change = c_ref[rows, :]
            q_ref[rows, :] = g_ref[rows, :] + RIDGE * change + sign * piece
            total = total + fold(piece * change)
        denom = denom + sign * total
    own = jnp.where(par == 0, squares[0], squares[1])
    numer = jnp.sum(own, axis=0, keepdims=True)
    denom = jnp.sum(denom, axis=0, keepdims=True) + RIDGE * numer
    rest = jnp.zeros((EXTRA - 2, c_ref.shape[1]), jnp.float32)
    near_ref[pl.ds(face, EXTRA), :] = jnp.concatenate([numer, denom, rest], axis=0)


def prep_kernel(k_hbm, rhs_hbm, flag_hbm, g_ref, lo_ref, held_ref, rhs_ref, flag_ref, sems):
    whole = pltpu.make_async_copy(k_hbm, held_ref, sems.at[0])
    rhs = pltpu.make_async_copy(rhs_hbm, rhs_ref, sems.at[1])
    flag = pltpu.make_async_copy(flag_hbm, flag_ref, sems.at[2])
    rhs.start()
    flag.start()
    whole.start()
    rhs.wait()
    flag.wait()
    set_face(rhs_ref, flag_ref, 0, g_ref, lo_ref)
    whole.wait()


def first_kernel(par_ref, live_ref, k_ref, own_g_ref, own_lo_ref, prev_ref, flag_prev_ref,
                 near_ref, far_ref, m_ref, q_ref, lo_ref, g_ref, c_ref, u_ref):
    par = par_ref[0, 0]
    live = live_ref[0, 0]
    face = prev_ref.shape[0]
    own = pl.ds(pl.multiple_of(face * par, face), face)
    g_ref[own, :] = own_g_ref[...]
    lo_ref[own, :] = own_lo_ref[...]
    set_face(prev_ref, flag_prev_ref, face * (1 - par), g_ref, lo_ref)
    squares = [jnp.zeros((8, prev_ref.shape[1]), jnp.float32) for _ in range(2)]
    for chunk in range(2 * face // CHUNK):
        rows = pl.ds(chunk * CHUNK, CHUNK)
        half = (chunk * CHUNK) // face
        change = jnp.maximum(-(FIRST_STEP * g_ref[rows, :]), lo_ref[rows, :].astype(jnp.float32))
        m_ref[rows, :] = change
        c_ref[rows, :] = change
        squares[half] = squares[half] + fold(change * change)
        store_operand(par, live, chunk, change, face, u_ref)
    product(par, live, squares, k_ref, u_ref, g_ref, c_ref, q_ref, near_ref, far_ref)


def pair_kernel(near_ref, got_ref, send_ref):
    rows = pl.ds(near_ref.shape[0] - EXTRA, EXTRA)
    both = near_ref[rows, :] + got_ref[rows, :]
    send_ref[...] = jnp.broadcast_to(both[None, 0:2, :], send_ref.shape)


def total_kernel(sums_ref, step_ref):
    total = sums_ref[...]
    count = total.shape[0]
    while count > 1:
        count //= 2
        total = total[:count] + total[count:]
    total = total[0]
    step_ref[...] = (total[0:1, :] + EPSILON) / (total[1:2, :] + EPSILON)


def step_kernel(last, par_ref, live_ref, k_ref, step_ref, near_got, far_got, m_in, q_in, lo_ref, *outs):
    if last:
        top_ref, base_ref, own_ref, u_ref, g_ref, m_ref, c_ref = outs
    else:
        near_ref, far_ref, m_ref, q_ref, g_ref, c_ref, u_ref = outs
    par = par_ref[0, 0]
    live = live_ref[0, 0]
    face = far_got.shape[0]
    step = step_ref[...]
    squares = [jnp.zeros((8, far_got.shape[1]), jnp.float32) for _ in range(2)]
    for chunk in range(2 * face // CHUNK):
        rows = pl.ds(chunk * CHUNK, CHUNK)
        half = (chunk * CHUNK) // face
        inner = pl.ds(chunk * CHUNK - half * face, CHUNK)
        got = (near_got, far_got)[half]
        grad = q_in[rows, :] - sign_of(par, half) * got[inner, :]
        g_ref[rows, :] = grad
        old = m_in[rows, :]
        moved = jnp.maximum(old - step * grad, lo_ref[rows, :].astype(jnp.float32))
        change = moved - old
        m_ref[rows, :] = moved
        c_ref[rows, :] = change
        if not last:
            squares[half] = squares[half] + fold(change * change)
        store_operand(par, live, chunk, change, face, u_ref)
    if not last:
        product(par, live, squares, k_ref, u_ref, g_ref, c_ref, q_ref, near_ref, far_ref)
        return
    operand = u_ref[...]
    for t in range(face // TILE):
        top_ref[pl.ds(t * TILE, TILE), :] = tile_product(t * TILE, live, k_ref, operand)
    own = pl.ds(pl.multiple_of(face * par, face), face)
    own_ref[...] = m_ref[own, :]
    base_ref[...] = g_ref[own, :] + RIDGE * c_ref[own, :]


def tail_kernel(live_ref, k_ref, u_ref, base_ref, own_ref, pre_ref, out_ref):
    face = base_ref.shape[0]
    operand = u_ref[...]
    out_ref[...] = own_ref[...]
    for t in range(face // TILE):
        rows = pl.ds(t * TILE, TILE)
        pre_ref[rows, :] = base_ref[rows, :] + tile_product(face + t * TILE, live_ref[0, 0], k_ref, operand)


def on_device(operators, dual_rhs, contact, costs, *, chips):
    matrix = pltpu.with_memory_space_constraint(operators[0, 0], pltpu.HBM)
    rhs = dual_rhs[0]
    face, cases = rhs.shape
    order = 2 * face
    wide = 2 * chips
    par = lax.axis_index("core").astype(jnp.int32).reshape(1, 1)
    forward = [(i, (i + 1) % wide) for i in range(wide)]
    backward = [((i + 1) % wide, i) for i in range(wide)]
    near_pairs = [(i, i ^ 1) for i in range(wide)]
    far_pairs = [(i, (i + 1) % wide if i % 2 else (i - 1) % wide) for i in range(wide)]

    rhs_prev = lax.ppermute(rhs, WIDE, forward)
    flag_prev = lax.ppermute(contact, WIDE, forward)

    f32, bf16 = jnp.float32, jnp.bfloat16
    send_s = jax.ShapeDtypeStruct((chips, 2, cases), f32)
    near_s = jax.ShapeDtypeStruct((face + EXTRA, cases), f32)
    half_s = jax.ShapeDtypeStruct((face, cases), f32)
    full_s = jax.ShapeDtypeStruct((order, cases), f32)
    low_s = jax.ShapeDtypeStruct((order, cases), bf16)
    full = pltpu.VMEM((order, cases), f32)
    operand = pltpu.VMEM((order, cases), bf16)
    call = functools.partial(
        pl.pallas_call,
        compiler_params=pltpu.CompilerParams(vmem_limit_bytes=16 << 20),
        cost_estimate=pl.CostEstimate(
            flops=2 * order * order * cases, bytes_accessed=2 * order * order, transcendentals=0
        ),
    )

    own_g, own_lo, held = call(
        prep_kernel,
        out_shape=(
            half_s,
            jax.ShapeDtypeStruct((face, cases), bf16),
            jax.ShapeDtypeStruct(matrix.shape, matrix.dtype),
        ),
        in_specs=[HBM] * 3,
        out_specs=(VMEM,) * 3,
        scratch_shapes=[
            pltpu.VMEM(rhs.shape, f32),
            pltpu.VMEM(contact.shape, contact.dtype),
            pltpu.SemaphoreType.DMA((3,)),
        ],
        name="prep",
    )(
        matrix,
        pltpu.with_memory_space_constraint(rhs, pltpu.HBM),
        pltpu.with_memory_space_constraint(contact, pltpu.HBM),
    )
    near, far, m, q, lo = call(
        first_kernel,
        out_shape=(near_s, half_s, full_s, full_s, low_s),
        in_specs=[SMEM, SMEM] + [VMEM] * 5,
        out_specs=(VMEM,) * 5,
        scratch_shapes=[full, full, operand],
        name="first",
    )(par, costs, held, own_g, own_lo, rhs_prev, flag_prev)

    for iteration in range(1, ITERS):
        last = iteration + 1 == ITERS
        near_got = lax.ppermute(near, WIDE, near_pairs)
        far_got = lax.ppermute(far, WIDE, far_pairs)
        send = call(
            pair_kernel,
            out_shape=send_s,
            in_specs=[VMEM, VMEM],
            out_specs=VMEM,
            name="pair",
        )(near, near_got)
        sums = lax.all_to_all(send, "chip", 0, 0)
        steplen = call(
            total_kernel,
            out_shape=jax.ShapeDtypeStruct((1, cases), f32),
            in_specs=[VMEM],
            out_specs=VMEM,
            name="total",
        )(sums)
        args = (par, costs, held, steplen, near_got, far_got, m, q, lo)
        if not last:
            near, far, m, q = call(
                functools.partial(step_kernel, False),
                out_shape=(near_s, half_s, full_s, full_s),
                in_specs=[SMEM, SMEM] + [VMEM] * 7,
                out_specs=(VMEM,) * 4,
                scratch_shapes=[full, full, operand],
                name="step",
            )(*args)
        else:
            top, base, own, u = call(
                functools.partial(step_kernel, True),
                out_shape=(half_s, half_s, half_s, low_s),
                in_specs=[SMEM, SMEM] + [VMEM] * 7,
                out_specs=(VMEM,) * 4,
                scratch_shapes=[full, full, full],
                name="last",
            )(*args)
    got = lax.ppermute(top, WIDE, backward)
    pre, own = call(
        tail_kernel,
        out_shape=(half_s, half_s),
        in_specs=[SMEM] + [VMEM] * 4,
        out_specs=(VMEM,) * 2,
        name="tail",
    )(costs, held, u, base, own)
    gradient = pre - got
    return own[None], gradient[None]


def solution(mesh):
    chips = mesh.shape["wide"] // 2
    finer = Mesh(mesh.devices.reshape(chips, 2, mesh.shape["lend"]), WIDE + ("lend",))
    return jax.shard_map(
        functools.partial(on_device, chips=chips),
        mesh=finer,
        in_specs=(
            P("lend", WIDE, None, None),
            P("lend", WIDE, None),
            P("lend", WIDE),
            P("lend", WIDE),
        ),
        out_specs=(P("lend", WIDE, None), P("lend", WIDE, None)),
        check_vma=False,
    )
```

profile of v0, /device:TPU:1, one launch (start us, length us, event | category | flops | bytes accessed | tf_op | source)
XLA Modules:
  0.0 106.3 jit_solution(158622630349696091)
XLA Ops:
  0.6 6.3 %collective-permute-start = (f32[512,128]{1,0:T(8,128)}, f32[512,128]{1,0:T(8,128)S(1)}, u32[]{:S(2)}, u32[]{:S(2)}) collective-permute-start(f32[512,128]{1,0:T(8,128)} %bitcast.7), channel_id=1, source_target_pairs={{0,8},{8,16},{16,24},{24,32},{32,40},{40,48},{48,56},{56,64},{64,7... | collective-permute-start | bytes 786440 | tf_op jit(solution)/shard_map/ppermute | solution.py:192
  6.9 1.9 %collective-permute-start.1 = (s32[1,512]{1,0:T(1,128)}, s32[1,512]{1,0:T(1,128)S(1)}, u32[]{:S(2)}, u32[]{:S(2)}) collective-permute-start(s32[1,512]{1,0:T(1,128)} %flag_hbm.1), channel_id=1, source_target_pairs={{0,8},{8,16},{16,24},{24,32},{32,40},{40,48},{48,56},{56,64},{64,7... | collective-permute-start | bytes 6152 | tf_op jit(solution)/shard_map/ppermute | solution.py:193
  8.9 1.7 %prep.1 = (f32[512,128]{1,0:T(8,128)S(1)}, bf16[512,128]{1,0:T(8,128)(2,1)S(1)}, bf16[1024,1024]{1,0:T(8,128)(2,1)S(1)}) custom-call(bf16[1024,1024]{1,0:T(8,128)(2,1)} %bitcast.6, f32[512,128]{1,0:T(8,128)} %bitcast.8, s32[1,512]{1,0:T(1,128)} %flag_hbm.1), custom_call_target="tpu_custom_call" | custom-call | flops 268435456 | bytes 2097152 | tf_op jit(solution)/shard_map/prep/pallas_call | solution.py:211
  11.2 8.2 %collective-permute-done.1.flag_prev_ref = s32[1,512]{1,0:T(1,128)S(1)} collective-permute-done((s32[1,512]{1,0:T(1,128)}, s32[1,512]{1,0:T(1,128)S(1)}, u32[]{:S(2)}, u32[]{:S(2)}) %collective-permute-start.1) | collective-permute-done | bytes 2080 | tf_op jit(solution)/shard_map/ppermute | solution.py:193
  19.4 0.0 collective-permute-done.prev_ref
  19.4 1.0 first.1
  20.5 8.5 %collective-permute-start.2 = (f32[520,128]{1,0:T(8,128)S(1)}, f32[520,128]{1,0:T(8,128)S(1)}, u32[]{:S(2)}, u32[]{:S(2)}) collective-permute-start(f32[520,128]{1,0:T(8,128)S(1)} %get-tuple-element.27.near_ref), channel_id=1, source_target_pairs={{0,8},{8,0},{16,24},{24,16},{32,40},{40,32},{48,56},{56,48},{64,72... | collective-permute-start | bytes 798728 | tf_op jit(solution)/shard_map/ppermute | solution.py:242
  28.9 1.9 %collective-permute-start.3 = (f32[512,128]{1,0:T(8,128)S(1)}, f32[512,128]{1,0:T(8,128)S(1)}, u32[]{:S(2)}, u32[]{:S(2)}) collective-permute-start(f32[512,128]{1,0:T(8,128)S(1)} %get-tuple-element.28), channel_id=1, source_target_pairs={{0,1016},{8,16},{16,8},{24,32},{32,24},{40,48},{48,40},{56,64},{64... | collective-permute-start | bytes 786440 | tf_op jit(solution)/shard_map/ppermute | solution.py:243
  30.9 0.0 collective-permute-done.2.got_ref.near_got
  30.9 19.4 %all_to_all.15.sums_ref = f32[64,2,128]{2,1,0:T(2,128)S(1)} all-to-all(f32[64,2,128]{2,1,0:T(2,128)S(1)} %pair.3), channel_id=1, replica_groups=mesh['chip'=64,'core'=2,'lend'=8] {'chip'}, dimensions={0} | all-to-all | bytes 131072 | tf_op jit(solution)/shard_map/all_to_all | solution.py:251
  50.3 0.0 collective-permute-done.3.far_got
  50.3 1.0 step.2
  51.3 2.3 %collective-permute-start.4 = (f32[520,128]{1,0:T(8,128)S(1)}, f32[520,128]{1,0:T(8,128)S(1)}, u32[]{:S(2)}, u32[]{:S(2)}) collective-permute-start(f32[520,128]{1,0:T(8,128)S(1)} %get-tuple-element.32.near_ref), channel_id=1, source_target_pairs={{0,8},{8,0},{16,24},{24,16},{32,40},{40,32},{48,56},{56,48},{64,72... | collective-permute-start | bytes 798728 | tf_op jit(solution)/shard_map/ppermute | solution.py:242
  53.6 2.3 %collective-permute-start.5 = (f32[512,128]{1,0:T(8,128)S(1)}, f32[512,128]{1,0:T(8,128)S(1)}, u32[]{:S(2)}, u32[]{:S(2)}) collective-permute-start(f32[512,128]{1,0:T(8,128)S(1)} %get-tuple-element.33), channel_id=1, source_target_pairs={{0,1016},{8,16},{16,8},{24,32},{32,24},{40,48},{48,40},{56,64},{64... | collective-permute-start | bytes 786440 | tf_op jit(solution)/shard_map/ppermute | solution.py:243
  55.9 0.0 collective-permute-done.4.got_ref.near_got
  55.9 17.9 %all_to_all.16.sums_ref = f32[64,2,128]{2,1,0:T(2,128)S(1)} all-to-all(f32[64,2,128]{2,1,0:T(2,128)S(1)} %pair.4), channel_id=1, replica_groups=mesh['chip'=64,'core'=2,'lend'=8] {'chip'}, dimensions={0} | all-to-all | bytes 131072 | tf_op jit(solution)/shard_map/all_to_all | solution.py:251
  73.9 0.0 collective-permute-done.5.far_got
  73.9 1.0 step.3
  74.8 1.9 %collective-permute-start.6 = (f32[520,128]{1,0:T(8,128)S(1)}, f32[520,128]{1,0:T(8,128)S(1)}, u32[]{:S(2)}, u32[]{:S(2)}) collective-permute-start(f32[520,128]{1,0:T(8,128)S(1)} %get-tuple-element.36.near_ref), channel_id=1, source_target_pairs={{0,8},{8,0},{16,24},{24,16},{32,40},{40,32},{48,56},{56,48},{64,72... | collective-permute-start | bytes 798728 | tf_op jit(solution)/shard_map/ppermute | solution.py:242
  76.8 2.6 %collective-permute-start.7 = (f32[512,128]{1,0:T(8,128)S(1)}, f32[512,128]{1,0:T(8,128)S(1)}, u32[]{:S(2)}, u32[]{:S(2)}) collective-permute-start(f32[512,128]{1,0:T(8,128)S(1)} %get-tuple-element.37), channel_id=1, source_target_pairs={{0,1016},{8,16},{16,8},{24,32},{32,24},{40,48},{48,40},{56,64},{64... | collective-permute-start | bytes 786440 | tf_op jit(solution)/shard_map/ppermute | solution.py:243
  79.4 0.0 collective-permute-done.6.got_ref.near_got
  79.5 17.7 %all_to_all.17.sums_ref = f32[64,2,128]{2,1,0:T(2,128)S(1)} all-to-all(f32[64,2,128]{2,1,0:T(2,128)S(1)} %pair.5), channel_id=1, replica_groups=mesh['chip'=64,'core'=2,'lend'=8] {'chip'}, dimensions={0} | all-to-all | bytes 131072 | tf_op jit(solution)/shard_map/all_to_all | solution.py:251
  97.2 0.0 collective-permute-done.7.far_got
  97.2 0.7 last.1
  97.9 1.9 %collective-permute-start.8 = (f32[512,128]{1,0:T(8,128)S(1)}, f32[512,128]{1,0:T(8,128)S(1)}, u32[]{:S(2)}, u32[]{:S(2)}) collective-permute-start(f32[512,128]{1,0:T(8,128)S(1)} %get-tuple-element.45), channel_id=1, source_target_pairs={{8,0},{16,8},{24,16},{32,24},{40,32},{48,40},{56,48},{64,56},{72,6... | collective-permute-start | bytes 786440 | tf_op jit(solution)/shard_map/ppermute | solution.py:278
  99.8 1.1 %tail.1 = (f32[512,128]{1,0:T(8,128)S(1)}, f32[512,128]{1,0:T(8,128)}) custom-call(s32[1,1]{1,0:T(1,128)S(6)} %copy.6.live_ref, bf16[1024,1024]{1,0:T(8,128)(2,1)S(1)} %get-tuple-element.24.k_ref, bf16[1024,128]{1,0:T(8,128)(2,1)S(1)} %get-tuple-element.40.u_ref, f32[512,128]{1,0:T(8,128)S(1)} %get-tuple-element.41.base_ref, ...), custom_call_target="tpu_custom_call" | custom-call | flops 268435456 | bytes 2097152 | tf_op jit(solution)/shard_map/tail/pallas_call | solution.py:279
  100.9 4.7 %collective-permute-done.8 = f32[512,128]{1,0:T(8,128)S(1)} collective-permute-done((f32[512,128]{1,0:T(8,128)S(1)}, f32[512,128]{1,0:T(8,128)S(1)}, u32[]{:S(2)}, u32[]{:S(2)}) %collective-permute-start.8) | collective-permute-done | bytes 262176 | tf_op jit(solution)/shard_map/ppermute | solution.py:278
  105.6 0.7 subtract_bitcast_fusion
  (6 shorter events, 0.1 us)
Async XLA Ops:
  0.6 18.8 %collective-permute-start = (f32[512,128]{1,0:T(8,128)}, f32[512,128]{1,0:T(8,128)S(1)}, u32[]{:S(2)}, u32[]{:S(2)}) collective-permute-start(f32[512,128]{1,0:T(8,128)} %bitcast.7), channel_id=1, source_target_pairs={{0,8},{8,16},{16,24},{24,32},{32,40},{40,48},{48,56},{56,64},{64,7... | collective-permute-start | bytes 786440 | tf_op jit(solution)/shard_map/ppermute | solution.py:192
  6.9 12.5 %collective-permute-start.1 = (s32[1,512]{1,0:T(1,128)}, s32[1,512]{1,0:T(1,128)S(1)}, u32[]{:S(2)}, u32[]{:S(2)}) collective-permute-start(s32[1,512]{1,0:T(1,128)} %flag_hbm.1), channel_id=1, source_target_pairs={{0,8},{8,16},{16,24},{24,32},{32,40},{40,48},{48,56},{56,64},{64,7... | collective-permute-start | bytes 6152 | tf_op jit(solution)/shard_map/ppermute | solution.py:193
  20.5 10.4 %collective-permute-start.2 = (f32[520,128]{1,0:T(8,128)S(1)}, f32[520,128]{1,0:T(8,128)S(1)}, u32[]{:S(2)}, u32[]{:S(2)}) collective-permute-start(f32[520,128]{1,0:T(8,128)S(1)} %get-tuple-element.27.near_ref), channel_id=1, source_target_pairs={{0,8},{8,0},{16,24},{24,16},{32,40},{40,32},{48,56},{56,48},{64,72... | collective-permute-start | bytes 798728 | tf_op jit(solution)/shard_map/ppermute | solution.py:242
  28.9 21.4 %collective-permute-start.3 = (f32[512,128]{1,0:T(8,128)S(1)}, f32[512,128]{1,0:T(8,128)S(1)}, u32[]{:S(2)}, u32[]{:S(2)}) collective-permute-start(f32[512,128]{1,0:T(8,128)S(1)} %get-tuple-element.28), channel_id=1, source_target_pairs={{0,1016},{8,16},{16,8},{24,32},{32,24},{40,48},{48,40},{56,64},{64... | collective-permute-start | bytes 786440 | tf_op jit(solution)/shard_map/ppermute | solution.py:243
  51.3 4.6 %collective-permute-start.4 = (f32[520,128]{1,0:T(8,128)S(1)}, f32[520,128]{1,0:T(8,128)S(1)}, u32[]{:S(2)}, u32[]{:S(2)}) collective-permute-start(f32[520,128]{1,0:T(8,128)S(1)} %get-tuple-element.32.near_ref), channel_id=1, source_target_pairs={{0,8},{8,0},{16,24},{24,16},{32,40},{40,32},{48,56},{56,48},{64,72... | collective-permute-start | bytes 798728 | tf_op jit(solution)/shard_map/ppermute | solution.py:242
  53.6 20.2 %collective-permute-start.5 = (f32[512,128]{1,0:T(8,128)S(1)}, f32[512,128]{1,0:T(8,128)S(1)}, u32[]{:S(2)}, u32[]{:S(2)}) collective-permute-start(f32[512,128]{1,0:T(8,128)S(1)} %get-tuple-element.33), channel_id=1, source_target_pairs={{0,1016},{8,16},{16,8},{24,32},{32,24},{40,48},{48,40},{56,64},{64... | collective-permute-start | bytes 786440 | tf_op jit(solution)/shard_map/ppermute | solution.py:243
  74.8 4.6 %collective-permute-start.6 = (f32[520,128]{1,0:T(8,128)S(1)}, f32[520,128]{1,0:T(8,128)S(1)}, u32[]{:S(2)}, u32[]{:S(2)}) collective-permute-start(f32[520,128]{1,0:T(8,128)S(1)} %get-tuple-element.36.near_ref), channel_id=1, source_target_pairs={{0,8},{8,0},{16,24},{24,16},{32,40},{40,32},{48,56},{56,48},{64,72... | collective-permute-start | bytes 798728 | tf_op jit(solution)/shard_map/ppermute | solution.py:242
  76.8 20.4 %collective-permute-start.7 = (f32[512,128]{1,0:T(8,128)S(1)}, f32[512,128]{1,0:T(8,128)S(1)}, u32[]{:S(2)}, u32[]{:S(2)}) collective-permute-start(f32[512,128]{1,0:T(8,128)S(1)} %get-tuple-element.37), channel_id=1, source_target_pairs={{0,1016},{8,16},{16,8},{24,32},{32,24},{40,48},{48,40},{56,64},{64... | collective-permute-start | bytes 786440 | tf_op jit(solution)/shard_map/ppermute | solution.py:243
  97.9 7.7 %collective-permute-start.8 = (f32[512,128]{1,0:T(8,128)S(1)}, f32[512,128]{1,0:T(8,128)S(1)}, u32[]{:S(2)}, u32[]{:S(2)}) collective-permute-start(f32[512,128]{1,0:T(8,128)S(1)} %get-tuple-element.45), channel_id=1, source_target_pairs={{8,0},{16,8},{24,16},{32,24},{40,32},{48,40},{56,48},{64,56},{72,6... | collective-permute-start | bytes 786440 | tf_op jit(solution)/shard_map/ppermute | solution.py:278
where the time goes:
time: 107 us; the launch traced here: 106 us
  blocking collectives  55 us (51%)
  starting transfers between devices  29.6 us (28%)
  waiting for transfers between devices  12.9 us (12%)
  Pallas kernels  6.59 us (6%)
  between operations  1.45 us (1%)
    all_to_all x3, blocking collectives, on_device(): sums = lax.all_to_all(send, 'chip', 0, 0)  55 us
    ppermute x3, starting transfers between devices, on_device(): near_got = lax.ppermute(near, WIDE, near_pairs)  12.7 us
    ppermute x1, waiting for transfers between devices, on_device(): flag_prev = lax.ppermute(contact, WIDE, forward)  8.2 us
    ppermute x3, starting transfers between devices, on_device(): far_got = lax.ppermute(far, WIDE, far_pairs)  6.83 us
    ppermute x1, starting transfers between devices, on_device(): rhs_prev = lax.ppermute(rhs, WIDE, forward)  6.29 us
    ppermute x1, waiting for transfers between devices, on_device(): got = lax.ppermute(top, WIDE, backward)  4.67 us
  transfers between devices with their start and end apart: 9, of which 2 were waited for; matrix products, arithmetic and copies ran while one was open for 0% of the time, Pallas kernels for 3%

commit v1 on v0

--- a/solution.py
+++ b/solution.py
@@ -70,7 +70,8 @@
         for t in range(face // TILE):
             piece = tile_product(base_of(par, half, face) + t * TILE, live, k_ref, operand)
             rows = pl.ds(half * face + t * TILE, TILE)
-            (near_ref, far_ref)[half][pl.ds(t * TILE, TILE), :] = piece
+            sent = (near_ref, far_ref)[half]
+            sent[pl.ds(t * TILE, TILE), :] = piece.astype(sent.dtype)
             change = c_ref[rows, :]
             q_ref[rows, :] = g_ref[rows, :] + RIDGE * change + sign * piece
             total = total + fold(piece * change)
@@ -147,7 +148,7 @@
         half = (chunk * CHUNK) // face
         inner = pl.ds(chunk * CHUNK - half * face, CHUNK)
         got = (near_got, far_got)[half]
-        grad = q_in[rows, :] - sign_of(par, half) * got[inner, :]
+        grad = q_in[rows, :] - sign_of(par, half) * got[inner, :].astype(jnp.float32)
         g_ref[rows, :] = grad
         old = m_in[rows, :]
         moved = jnp.maximum(old - step * grad, lo_ref[rows, :].astype(jnp.float32))
@@ -162,7 +163,8 @@
         return
     operand = u_ref[...]
     for t in range(face // TILE):
-        top_ref[pl.ds(t * TILE, TILE), :] = tile_product(t * TILE, live, k_ref, operand)
+        piece = tile_product(t * TILE, live, k_ref, operand)
+        top_ref[pl.ds(t * TILE, TILE), :] = piece.astype(top_ref.dtype)
     own = pl.ds(pl.multiple_of(face * par, face), face)
     own_ref[...] = m_ref[own, :]
     base_ref[...] = g_ref[own, :] + RIDGE * c_ref[own, :]
@@ -195,6 +197,7 @@
     f32, bf16 = jnp.float32, jnp.bfloat16
     send_s = jax.ShapeDtypeStruct((chips, 2, cases), f32)
     near_s = jax.ShapeDtypeStruct((face + EXTRA, cases), f32)
+    far_s = jax.ShapeDtypeStruct((face, cases), bf16)
     half_s = jax.ShapeDtypeStruct((face, cases), f32)
     full_s = jax.ShapeDtypeStruct((order, cases), f32)
     low_s = jax.ShapeDtypeStruct((order, cases), bf16)
@@ -230,7 +233,7 @@
     )
     near, far, m, q, lo = call(
         first_kernel,
-        out_shape=(near_s, half_s, full_s, full_s, low_s),
+        out_shape=(near_s, far_s, full_s, full_s, low_s),
         in_specs=[SMEM, SMEM] + [VMEM] * 5,
         out_specs=(VMEM,) * 5,
         scratch_shapes=[full, full, operand],
@@ -260,7 +263,7 @@
         if not last:
             near, far, m, q = call(
                 functools.partial(step_kernel, False),
-                out_shape=(near_s, half_s, full_s, full_s),
+                out_shape=(near_s, far_s, full_s, full_s),
                 in_specs=[SMEM, SMEM] + [VMEM] * 7,
                 out_specs=(VMEM,) * 4,
                 scratch_shapes=[full, full, operand],
@@ -283,7 +286,7 @@
         out_specs=(VMEM,) * 2,
         name="tail",
     )(costs, held, u, base, own)
-    gradient = pre - got
+    gradient = pre - got.astype(f32)
     return own[None], gradient[None]
 
 

time: 107 us -> 124 us (1.16)
  blocking collectives: 55 us -> 0 us
  starting transfers between devices: 29.6 us -> 61.1 us
  waiting for transfers between devices: 12.9 us -> 36.2 us
  local copies, waits for them, and re-layouts: 0 us -> 13.9 us
  Pallas kernels: 6.59 us -> 10.1 us
    all_to_all x3 -> x0, blocking collectives: 55 us -> none  [on_device(): sums = lax.all_to_all(send, 'chip', 0, 0)]
    all_to_all x0 -> x3, starting transfers between devices: none -> 22.4 us  [on_device(): sums = lax.all_to_all(send, 'chip', 0, 0)]
    all_to_all x0 -> x3, waiting for transfers between devices: none -> 22.1 us  [on_device(): sums = lax.all_to_all(send, 'chip', 0, 0)]
    unnamed x0 -> x34, local copies, waits for them, and re-layouts: none -> 13.9 us
    ppermute x3, starting transfers between devices: 6.83 us -> 11.1 us  [on_device(): far_got = lax.ppermute(far, WIDE, far_pairs)]
    ppermute x3, waiting for transfers between devices: 0.01 us -> 3.44 us  [on_device(): near_got = lax.ppermute(near, WIDE, near_pairs)]
    ppermute x3, starting transfers between devices: 12.7 us -> 15.8 us  [on_device(): near_got = lax.ppermute(near, WIDE, near_pairs)]
    pallas_call x3, Pallas kernels: 0.06 us -> 1.94 us  [on_device(): call(pair_kernel, out_shape=send_s, in_specs=[VMEM, VMEM], out_specs=VMEM...]
  transfers between devices with their start and end apart: 9 -> 12, of which waited for: 2 -> 8; matrix products, arithmetic and copies ran while one was open for 0% -> 0% of each run, Pallas kernels for 3% -> 4%
where the time goes in v1:
time: 124 us
  starting transfers between devices  61.1 us (49%)
  waiting for transfers between devices  36.2 us (29%)
  local copies, waits for them, and re-layouts  13.9 us (11%)
  Pallas kernels  10.1 us (8%)
  between operations  1.5 us (1%)
    all_to_all x3, starting transfers between devices, on_device(): sums = lax.all_to_all(send, 'chip', 0, 0)  22.4 us
    all_to_all x3, waiting for transfers between devices, on_device(): sums = lax.all_to_all(send, 'chip', 0, 0)  22.1 us
    ppermute x3, starting transfers between devices, on_device(): near_got = lax.ppermute(near, WIDE, near_pairs)  15.8 us
    unnamed x34, local copies, waits for them, and re-layouts  13.9 us
    ppermute x3, starting transfers between devices, on_device(): far_got = lax.ppermute(far, WIDE, far_pairs)  11.1 us
    ppermute x1, waiting for transfers between devices, on_device(): flag_prev = lax.ppermute(contact, WIDE, forward)  7.49 us
    ppermute x1, starting transfers between devices, on_device(): rhs_prev = lax.ppermute(rhs, WIDE, forward)  6.29 us
    ppermute x1, starting transfers between devices, on_device(): got = lax.ppermute(top, WIDE, backward)  3.68 us
  transfers between devices with their start and end apart: 12, of which 8 were waited for; matrix products, arithmetic and copies ran while one was open for 0% of the time, Pallas kernels for 4%

profile of v1, /device:TPU:1, one launch (start us, length us, event | category | flops | bytes accessed | tf_op | source)
XLA Modules:
  0.0 123.5 jit_solution(6168146863362742621)
XLA Ops:
  0.6 6.3 %collective-permute-start = (f32[512,128]{1,0:T(8,128)}, f32[512,128]{1,0:T(8,128)S(1)}, u32[]{:S(2)}, u32[]{:S(2)}) collective-permute-start(f32[512,128]{1,0:T(8,128)} %bitcast.7), channel_id=1, source_target_pairs={{0,8},{8,16},{16,24},{24,32},{32,40},{40,48},{48,56},{56,64},{64,7... | collective-permute-start | bytes 786440 | tf_op jit(solution)/shard_map/ppermute | solution.py:194
  6.9 1.9 %collective-permute-start.1 = (s32[1,512]{1,0:T(1,128)}, s32[1,512]{1,0:T(1,128)S(1)}, u32[]{:S(2)}, u32[]{:S(2)}) collective-permute-start(s32[1,512]{1,0:T(1,128)} %flag_hbm.1), channel_id=1, source_target_pairs={{0,8},{8,16},{16,24},{24,32},{32,40},{40,48},{48,56},{56,64},{64,7... | collective-permute-start | bytes 6152 | tf_op jit(solution)/shard_map/ppermute | solution.py:195
  8.9 1.7 %prep.1 = (f32[512,128]{1,0:T(8,128)S(1)}, bf16[512,128]{1,0:T(8,128)(2,1)S(1)}, bf16[1024,1024]{1,0:T(8,128)(2,1)S(1)}) custom-call(bf16[1024,1024]{1,0:T(8,128)(2,1)} %bitcast.6, f32[512,128]{1,0:T(8,128)} %bitcast.8, s32[1,512]{1,0:T(1,128)} %flag_hbm.1), custom_call_target="tpu_custom_call" | custom-call | flops 268435456 | bytes 2097152 | tf_op jit(solution)/shard_map/prep/pallas_call | solution.py:214
  12.0 7.5 %collective-permute-done.1.flag_prev_ref = s32[1,512]{1,0:T(1,128)S(1)} collective-permute-done((s32[1,512]{1,0:T(1,128)}, s32[1,512]{1,0:T(1,128)S(1)}, u32[]{:S(2)}, u32[]{:S(2)}) %collective-permute-start.1) | collective-permute-done | bytes 2080 | tf_op jit(solution)/shard_map/ppermute | solution.py:195
  20.2 0.9 copy-done.11
  21.1 0.9 copy-done.13
  22.1 1.0 first.1
  23.7 8.4 %collective-permute-start.2 = (f32[520,128]{1,0:T(8,128)S(1)}, f32[520,128]{1,0:T(8,128)S(1)}, u32[]{:S(2)}, u32[]{:S(2)}) collective-permute-start(f32[520,128]{1,0:T(8,128)S(1)} %get-tuple-element.27.near_ref), channel_id=1, source_target_pairs={{0,8},{8,0},{16,24},{24,16},{32,40},{40,32},{48,56},{56,48},{64,72... | collective-permute-start | bytes 798728 | tf_op jit(solution)/shard_map/ppermute | solution.py:245
  32.2 1.1 collective-permute-done.2.got_ref.near_got
  34.7 7.3 %all-to-all-start = ((f32[64,2,128]{2,1,0:T(2,128)}), f32[64,2,128]{2,1,0:T(2,128)}, u32[]{:S(2)}, u32[]{:S(2)}) async-start(f32[64,2,128]{2,1,0:T(2,128)} %pair.3), calls=%async_computation | async-start | bytes 131072 | tf_op jit(solution)/shard_map/all_to_all | solution.py:254
  41.9 3.7 %collective-permute-start.3 = (bf16[512,128]{1,0:T(8,128)(2,1)}, bf16[512,128]{1,0:T(8,128)(2,1)S(1)}, u32[]{:S(2)}, u32[]{:S(2)}) collective-permute-start(bf16[512,128]{1,0:T(8,128)(2,1)} %copy-done.14), channel_id=1, source_target_pairs={{0,1016},{8,16},{16,8},{24,32},{32,24},{40,48},{48,40},{56,64},{64... | collective-permute-start | bytes 393224 | tf_op jit(solution)/shard_map/ppermute | solution.py:246
  45.6 7.3 %all-to-all-done.sums_ref = f32[64,2,128]{2,1,0:T(2,128)} async-done(((f32[64,2,128]{2,1,0:T(2,128)}), f32[64,2,128]{2,1,0:T(2,128)}, u32[]{:S(2)}, u32[]{:S(2)}) %all-to-all-start) | async-done | bytes 65568 | tf_op jit(solution)/shard_map/all_to_all | solution.py:254
  53.8 0.9 copy-done.7
  54.8 1.0 step.2
  58.0 3.7 %collective-permute-start.4 = (f32[520,128]{1,0:T(8,128)S(1)}, f32[520,128]{1,0:T(8,128)S(1)}, u32[]{:S(2)}, u32[]{:S(2)}) collective-permute-start(f32[520,128]{1,0:T(8,128)S(1)} %get-tuple-element.32.near_ref), channel_id=1, source_target_pairs={{0,8},{8,0},{16,24},{24,16},{32,40},{40,32},{48,56},{56,48},{64,72... | collective-permute-start | bytes 798728 | tf_op jit(solution)/shard_map/ppermute | solution.py:245
  61.6 1.1 collective-permute-done.4.got_ref.near_got
  64.1 7.1 %all-to-all-start.1 = ((f32[64,2,128]{2,1,0:T(2,128)}), f32[64,2,128]{2,1,0:T(2,128)S(1)}, u32[]{:S(2)}, u32[]{:S(2)}) async-start(f32[64,2,128]{2,1,0:T(2,128)} %pair.4), calls=%async_computation.1 | async-start | bytes 131072 | tf_op jit(solution)/shard_map/all_to_all | solution.py:254
  71.2 3.7 %collective-permute-start.5 = (bf16[512,128]{1,0:T(8,128)(2,1)}, bf16[512,128]{1,0:T(8,128)(2,1)S(1)}, u32[]{:S(2)}, u32[]{:S(2)}) collective-permute-start(bf16[512,128]{1,0:T(8,128)(2,1)} %copy-done.15), channel_id=1, source_target_pairs={{0,1016},{8,16},{16,8},{24,32},{32,24},{40,48},{48,40},{56,64},{64... | collective-permute-start | bytes 393224 | tf_op jit(solution)/shard_map/ppermute | solution.py:246
  75.0 7.4 %all-to-all-done.1.sums_ref = f32[64,2,128]{2,1,0:T(2,128)S(1)} async-done(((f32[64,2,128]{2,1,0:T(2,128)}), f32[64,2,128]{2,1,0:T(2,128)S(1)}, u32[]{:S(2)}, u32[]{:S(2)}) %all-to-all-start.1) | async-done | bytes 65568 | tf_op jit(solution)/shard_map/all_to_all | solution.py:254
  82.4 1.0 copy-done.1
  83.4 1.0 copy-done.3
  84.5 0.9 copy-done.9
  85.4 1.0 step.3
  87.0 3.7 %collective-permute-start.6 = (f32[520,128]{1,0:T(8,128)S(1)}, f32[520,128]{1,0:T(8,128)S(1)}, u32[]{:S(2)}, u32[]{:S(2)}) collective-permute-start(f32[520,128]{1,0:T(8,128)S(1)} %get-tuple-element.36.near_ref), channel_id=1, source_target_pairs={{0,8},{8,0},{16,24},{24,16},{32,40},{40,32},{48,56},{56,48},{64,72... | collective-permute-start | bytes 798728 | tf_op jit(solution)/shard_map/ppermute | solution.py:245
  90.7 1.1 collective-permute-done.6.got_ref.near_got
  93.2 8.1 %all-to-all-start.2 = ((f32[64,2,128]{2,1,0:T(2,128)}), f32[64,2,128]{2,1,0:T(2,128)}, u32[]{:S(2)}, u32[]{:S(2)}) async-start(f32[64,2,128]{2,1,0:T(2,128)} %pair.5), calls=%async_computation.2 | async-start | bytes 131072 | tf_op jit(solution)/shard_map/all_to_all | solution.py:254
  101.3 3.7 %collective-permute-start.7 = (bf16[512,128]{1,0:T(8,128)(2,1)}, bf16[512,128]{1,0:T(8,128)(2,1)S(1)}, u32[]{:S(2)}, u32[]{:S(2)}) collective-permute-start(bf16[512,128]{1,0:T(8,128)(2,1)} %copy-done.16), channel_id=1, source_target_pairs={{0,1016},{8,16},{16,8},{24,32},{32,24},{40,48},{48,40},{56,64},{64... | collective-permute-start | bytes 393224 | tf_op jit(solution)/shard_map/ppermute | solution.py:246
  105.0 7.3 %all-to-all-done.2.sums_ref = f32[64,2,128]{2,1,0:T(2,128)} async-done(((f32[64,2,128]{2,1,0:T(2,128)}), f32[64,2,128]{2,1,0:T(2,128)}, u32[]{:S(2)}, u32[]{:S(2)}) %all-to-all-start.2) | async-done | bytes 65568 | tf_op jit(solution)/shard_map/all_to_all | solution.py:254
  113.2 0.9 copy-done.5
  114.8 3.7 %collective-permute-start.8 = (f32[512,128]{1,0:T(8,128)S(1)}, f32[512,128]{1,0:T(8,128)S(1)}, u32[]{:S(2)}, u32[]{:S(2)}) collective-permute-start(f32[512,128]{1,0:T(8,128)S(1)} %get-tuple-element.45), channel_id=1, source_target_pairs={{8,0},{16,8},{24,16},{32,24},{40,32},{48,40},{56,48},{64,56},{72,6... | collective-permute-start | bytes 786440 | tf_op jit(solution)/shard_map/ppermute | solution.py:281
  118.5 1.1 tail.1
  119.6 3.2 %collective-permute-done.8 = f32[512,128]{1,0:T(8,128)S(1)} collective-permute-done((f32[512,128]{1,0:T(8,128)S(1)}, f32[512,128]{1,0:T(8,128)S(1)}, u32[]{:S(2)}, u32[]{:S(2)}) %collective-permute-start.8) | collective-permute-done | bytes 262176 | tf_op jit(solution)/shard_map/ppermute | solution.py:281
  (39 shorter events, 12.2 us)
Async XLA Ops:
  0.6 18.8 %collective-permute-start = (f32[512,128]{1,0:T(8,128)}, f32[512,128]{1,0:T(8,128)S(1)}, u32[]{:S(2)}, u32[]{:S(2)}) collective-permute-start(f32[512,128]{1,0:T(8,128)} %bitcast.7), channel_id=1, source_target_pairs={{0,8},{8,16},{16,24},{24,32},{32,40},{40,48},{48,56},{56,64},{64,7... | collective-permute-start | bytes 786440 | tf_op jit(solution)/shard_map/ppermute | solution.py:194
  6.9 12.5 %collective-permute-start.1 = (s32[1,512]{1,0:T(1,128)}, s32[1,512]{1,0:T(1,128)S(1)}, u32[]{:S(2)}, u32[]{:S(2)}) collective-permute-start(s32[1,512]{1,0:T(1,128)} %flag_hbm.1), channel_id=1, source_target_pairs={{0,8},{8,16},{16,24},{24,32},{32,40},{40,48},{48,56},{56,64},{64,7... | collective-permute-start | bytes 6152 | tf_op jit(solution)/shard_map/ppermute | solution.py:195
  10.6 0.7 copy-start.12
  19.4 0.7 copy-start.10
  20.1 0.9 copy-start.11
  21.1 0.9 copy-start.13
  23.1 0.7 copy-start.14
  23.7 9.6 %collective-permute-start.2 = (f32[520,128]{1,0:T(8,128)S(1)}, f32[520,128]{1,0:T(8,128)S(1)}, u32[]{:S(2)}, u32[]{:S(2)}) collective-permute-start(f32[520,128]{1,0:T(8,128)S(1)} %get-tuple-element.27.near_ref), channel_id=1, source_target_pairs={{0,8},{8,0},{16,24},{24,16},{32,40},{40,32},{48,56},{56,48},{64,72... | collective-permute-start | bytes 798728 | tf_op jit(solution)/shard_map/ppermute | solution.py:245
  34.0 0.7 copy-start.6
  34.7 18.3 %all-to-all-start = ((f32[64,2,128]{2,1,0:T(2,128)}), f32[64,2,128]{2,1,0:T(2,128)}, u32[]{:S(2)}, u32[]{:S(2)}) async-start(f32[64,2,128]{2,1,0:T(2,128)} %pair.3), calls=%async_computation | async-start | bytes 131072 | tf_op jit(solution)/shard_map/all_to_all | solution.py:254
  41.9 11.9 %collective-permute-start.3 = (bf16[512,128]{1,0:T(8,128)(2,1)}, bf16[512,128]{1,0:T(8,128)(2,1)S(1)}, u32[]{:S(2)}, u32[]{:S(2)}) collective-permute-start(bf16[512,128]{1,0:T(8,128)(2,1)} %copy-done.14), channel_id=1, source_target_pairs={{0,1016},{8,16},{16,8},{24,32},{32,24},{40,48},{48,40},{56,64},{64... | collective-permute-start | bytes 393224 | tf_op jit(solution)/shard_map/ppermute | solution.py:246
  53.8 1.0 copy-start.7
  55.7 0.8 copy-start
  56.5 0.8 copy-start.2
  57.3 0.7 copy-start.15
  58.0 4.8 %collective-permute-start.4 = (f32[520,128]{1,0:T(8,128)S(1)}, f32[520,128]{1,0:T(8,128)S(1)}, u32[]{:S(2)}, u32[]{:S(2)}) collective-permute-start(f32[520,128]{1,0:T(8,128)S(1)} %get-tuple-element.32.near_ref), channel_id=1, source_target_pairs={{0,8},{8,0},{16,24},{24,16},{32,40},{40,32},{48,56},{56,48},{64,72... | collective-permute-start | bytes 798728 | tf_op jit(solution)/shard_map/ppermute | solution.py:245
  63.4 0.7 copy-start.8
  64.1 18.2 %all-to-all-start.1 = ((f32[64,2,128]{2,1,0:T(2,128)}), f32[64,2,128]{2,1,0:T(2,128)S(1)}, u32[]{:S(2)}, u32[]{:S(2)}) async-start(f32[64,2,128]{2,1,0:T(2,128)} %pair.4), calls=%async_computation.1 | async-start | bytes 131072 | tf_op jit(solution)/shard_map/all_to_all | solution.py:254
  71.2 11.2 %collective-permute-start.5 = (bf16[512,128]{1,0:T(8,128)(2,1)}, bf16[512,128]{1,0:T(8,128)(2,1)S(1)}, u32[]{:S(2)}, u32[]{:S(2)}) collective-permute-start(bf16[512,128]{1,0:T(8,128)(2,1)} %copy-done.15), channel_id=1, source_target_pairs={{0,1016},{8,16},{16,8},{24,32},{32,24},{40,48},{48,40},{56,64},{64... | collective-permute-start | bytes 393224 | tf_op jit(solution)/shard_map/ppermute | solution.py:246
  82.4 1.0 copy-start.1
  83.4 1.0 copy-start.3
  84.5 1.0 copy-start.9
  86.4 0.7 copy-start.16
  87.0 4.8 %collective-permute-start.6 = (f32[520,128]{1,0:T(8,128)S(1)}, f32[520,128]{1,0:T(8,128)S(1)}, u32[]{:S(2)}, u32[]{:S(2)}) collective-permute-start(f32[520,128]{1,0:T(8,128)S(1)} %get-tuple-element.36.near_ref), channel_id=1, source_target_pairs={{0,8},{8,0},{16,24},{24,16},{32,40},{40,32},{48,56},{56,48},{64,72... | collective-permute-start | bytes 798728 | tf_op jit(solution)/shard_map/ppermute | solution.py:245
  92.5 0.7 copy-start.4
  93.2 19.1 %all-to-all-start.2 = ((f32[64,2,128]{2,1,0:T(2,128)}), f32[64,2,128]{2,1,0:T(2,128)}, u32[]{:S(2)}, u32[]{:S(2)}) async-start(f32[64,2,128]{2,1,0:T(2,128)} %pair.5), calls=%async_computation.2 | async-start | bytes 131072 | tf_op jit(solution)/shard_map/all_to_all | solution.py:254
  101.3 11.9 %collective-permute-start.7 = (bf16[512,128]{1,0:T(8,128)(2,1)}, bf16[512,128]{1,0:T(8,128)(2,1)S(1)}, u32[]{:S(2)}, u32[]{:S(2)}) collective-permute-start(bf16[512,128]{1,0:T(8,128)(2,1)} %copy-done.16), channel_id=1, source_target_pairs={{0,1016},{8,16},{16,8},{24,32},{32,24},{40,48},{48,40},{56,64},{64... | collective-permute-start | bytes 393224 | tf_op jit(solution)/shard_map/ppermute | solution.py:246
  113.2 1.0 copy-start.5
  114.8 8.0 %collective-permute-start.8 = (f32[512,128]{1,0:T(8,128)S(1)}, f32[512,128]{1,0:T(8,128)S(1)}, u32[]{:S(2)}, u32[]{:S(2)}) collective-permute-start(f32[512,128]{1,0:T(8,128)S(1)} %get-tuple-element.45), channel_id=1, source_target_pairs={{8,0},{16,8},{24,16},{32,24},{40,32},{48,40},{56,48},{64,56},{72,6... | collective-permute-start | bytes 786440 | tf_op jit(solution)/shard_map/ppermute | solution.py:281
